TPU v7x, 512 devices: a whole 4x8x8 slice. The times are simulated.
512 devices in a mesh: stream: 8 (over y), span: 16 (over z, core), vert: 4 (over x).
Axes of the slice: x: 4, y: 8, z: 8, core: 2. Of those that a mesh axis runs over, the one named last changes fastest.
Arguments:
- fields: float32 [5, 128, 256, 1024], P(None, 'vert', 'span', 'stream'), may hold values from -6 to 6
- solid_frac: float32 [128, 256, 1024], P('vert', 'span', 'stream'), may hold values from 0 to 1
- panels: float32 [32768, 5, 256], P(('stream', 'span', 'vert')), may hold values from -0.015625 to 0.015625
- panel_owner: int32 [32768, 1], P(('stream', 'span', 'vert')), may hold values from 0 to 63; in each aligned block of 64 rows (0 to 63, 64 to 127, ...) at most 2 rows name the same one
- deck_cells: int32 [4, 16, 8, 2048], P('vert', 'span', 'stream'), may hold values from 0 to 65535
- deck_geom: float32 [4, 16, 8, 3, 2048], P('vert', None, 'stream'), may hold values from -6 to 6
- strip_ids: int32 [4, 16, 8, 2048], P('vert', None, 'stream'), may hold values from 0 to 63, as said below
- mode_shapes: float32 [3, 64, 32], replicated, may hold values from -0.0034179688 to 0.0034179688
Outputs:
- new_fields: float32 [5, 128, 256, 1024], P(None, 'vert', 'span', 'stream')
- modal_force: float32 [32], replicated
Inputs may be any that keep to these rules, and one draw needn't show every extreme that they name: `panel_owner`: tile number s * 4 + v for along-deck tile s and vertical tile v. Among the 64 panels of one device no tile is named more than 2 times; some device names some tile exactly 2 times. `strip_ids`: cells of along-deck tile s belong to strips s * 4 to (s + 1) * 4 - 1.
All inputs are finite; a program needn't handle non-finite values.
Results may differ from a plain program's by a relative error of at most 0.00012.
Values sent between devices are 32-bit elements; how exact they have to be, the bound alone decides.
No kernel may reach another device: no remote copies, remote signals or barrier semaphores. Data moves between devices by JAX's collectives and lax.ppermute only.
A program may use at most 128 MiB of HBM per device.

v0:
```python
import math
import jax
import jax.numpy as jnp
from jax import lax
from jax.sharding import PartitionSpec as P

CAP = 2
time_step = 0.15
viscous = 0.05
heat_diff = 0.03
sound_sq = 1.0
buoyant = 0.5
penalty = 0.5
relax_time = 0.5
relax_depth = 8.0
wave_cols = 16


def extended(block, sides, width):
    for axis, dim in sides:
        count = lax.axis_size(axis)
        forward = [(i, i + 1) for i in range(count - 1)]
        backward = [(target, source) for source, target in forward]
        low = lax.ppermute(
            lax.slice_in_dim(block, block.shape[dim] - width, None, axis=dim), axis, forward
        )
        high = lax.ppermute(lax.slice_in_dim(block, 0, width, axis=dim), axis, backward)
        block = jnp.concatenate([low, block, high], axis=dim)
    return block


def wave_basis(heights, widths, total_z, total_y, spec):
    modes = jnp.arange(spec, dtype=jnp.int32)
    across = (modes % wave_cols)[:, None, None]
    upward = (modes // wave_cols)[:, None, None]
    period = total_y * total_z
    phase = (
        across * widths[None, None, :] * total_z + upward * heights[None, :, None] * total_y
    ) % period
    angle = phase.astype(jnp.float32) * (2.0 * math.pi / period)
    return jnp.concatenate([jnp.cos(angle), jnp.sin(angle)], axis=0)


def relax_weights(positions, limit):
    spots = positions.astype(jnp.float32)
    return jnp.where(positions < limit, jnp.exp(-spots / relax_depth) / relax_time, 0.0)


def rates(padded, solid_frac, relax_rate, target_plane):
    centre = padded[:, 1:-1, 1:-1, 1:-1]
    east_side = padded[:, 1:-1, 1:-1, 2:]
    west_side = padded[:, 1:-1, 1:-1, :-2]
    north_side = padded[:, 1:-1, 2:, 1:-1]
    south_side = padded[:, 1:-1, :-2, 1:-1]
    upper_side = padded[:, 2:, 1:-1, 1:-1]
    lower_side = padded[:, :-2, 1:-1, 1:-1]
    grad_x = 0.5 * (east_side - west_side)
    grad_y = 0.5 * (north_side - south_side)
    grad_z = 0.5 * (upper_side - lower_side)
    laplace = (
        east_side + west_side + north_side + south_side + upper_side + lower_side - 6.0 * centre
    )
    speed_x = centre[0]
    speed_y = centre[1]
    speed_z = centre[2]
    carried = speed_x * grad_x + speed_y * grad_y + speed_z * grad_z
    coeffs = jnp.array([viscous, viscous, viscous, viscous, heat_diff], jnp.float32)[
        :, None, None, None
    ]
    damping = solid_frac / penalty
    nudging = relax_rate[None, None, None, :] * (target_plane[:, :, :, None] - centre)
    common = coeffs * laplace - carried + nudging
    extra_terms = jnp.stack(
        [
            -grad_x[3] - damping * speed_x,
            -grad_y[3] - damping * speed_y,
            -grad_z[3] - damping * speed_z + buoyant * centre[4],
            -sound_sq * (grad_x[0] + grad_y[1] + grad_z[2]),
            jnp.zeros_like(speed_x),
        ]
    )
    return common + extra_terms


def pack_slots(flat_panels, target_tile, chosen, tile_count):
    running = jnp.cumsum(chosen, axis=0) - 1
    slot_rank = jnp.sum(chosen * running, axis=1)
    slot_index = target_tile * CAP + slot_rank
    dispatch = (
        slot_index[None, :] == jnp.arange(tile_count * CAP, dtype=jnp.int32)[:, None]
    ).astype(jnp.float32)
    return jnp.dot(dispatch, flat_panels, precision=lax.Precision.HIGHEST)


def strip_forces(traction, labels, strip_count):
    columns = jnp.arange(strip_count, dtype=jnp.int32)

    def add_row(running, item_pair):
        row_values, row_labels = item_pair
        member = (row_labels[:, None] == columns[None, :]).astype(jnp.float32)
        return (running + jnp.dot(row_values, member, precision=lax.Precision.HIGHEST), None)

    start_value = jnp.zeros((traction.shape[1], strip_count), jnp.float32)
    summed, ignored = lax.scan(add_row, start_value, (traction, labels))
    return summed


def on_device(
    fields, solid_frac, panels, panel_owner, deck_cells, deck_geom, strip_ids, mode_shapes
):
    depth_cells = fields.shape[1]
    span_cells = fields.shape[2]
    wind_cells = fields.shape[3]
    n_span = lax.axis_size("span")
    n_vert = lax.axis_size("vert")
    stream_pos = lax.axis_index("stream")
    span_pos = lax.axis_index("span")
    vert_pos = lax.axis_index("vert")
    tile_count = n_span * n_vert
    held_panels = panels.shape[0]
    spec_cols = panels.shape[2]
    flat_panels = panels.reshape(held_panels, 5 * spec_cols)
    target_tile = panel_owner[:, 0]
    chosen = (target_tile[:, None] == jnp.arange(tile_count, dtype=jnp.int32)[None, :]).astype(
        jnp.int32
    )
    outgoing = pack_slots(flat_panels, target_tile, chosen, tile_count)
    arrived = lax.all_to_all(
        outgoing.reshape(tile_count, CAP * 5 * spec_cols),
        ("span", "vert"),
        split_axis=0,
        concat_axis=0,
        tiled=True,
    )
    coeffs = jnp.sum(arrived.reshape(-1, 5 * spec_cols), axis=0)
    coeffs = coeffs.reshape(5, spec_cols)
    heights = vert_pos * depth_cells + jnp.arange(depth_cells, dtype=jnp.int32)
    widths = span_pos * span_cells + jnp.arange(span_cells, dtype=jnp.int32)
    wave_table = wave_basis(
        heights, widths, depth_cells * n_vert, span_cells * n_span, spec_cols // 2
    )
    wave_table = wave_table.reshape(spec_cols, depth_cells * span_cells)
    partial_value = jnp.dot(coeffs, wave_table, precision=lax.Precision.HIGHEST)
    inflow_plane = lax.psum(partial_value, "stream").reshape(5, depth_cells, span_cells)
    target_plane = inflow_plane + jnp.array([1.0, 0.0, 0.0, 0.0, 0.0], jnp.float32)[:, None, None]
    wind_first = stream_pos * wind_cells
    relax_rate = relax_weights(
        wind_first + jnp.arange(wind_cells, dtype=jnp.int32), wind_cells // 2
    )

    def advance(state):
        padded = extended(state, (("stream", 3), ("span", 2), ("vert", 1)), 1)
        return rates(padded, solid_frac, relax_rate, target_plane)

    first_update = fields + time_step * advance(fields)
    second_rate = advance(first_update)
    new_fields = 0.5 * (fields + first_update + time_step * second_rate)
    pressure = new_fields[3].reshape(-1)
    sampled = pressure[deck_cells[0, 0, 0]]
    strip_count = mode_shapes.shape[1]
    rows_all = lax.all_gather(sampled.reshape(1, 1, 1, -1), "span", axis=1, tiled=True)
    traction = rows_all[0, :, 0][:, None, :] * deck_geom[0, :, 0]
    forces = strip_forces(traction, strip_ids[0, :, 0], strip_count)
    modal_part = jnp.einsum("cj,cjm->m", forces, mode_shapes, precision=lax.Precision.HIGHEST)
    modal_force = lax.psum(modal_part, ("stream", "vert"))
    return (new_fields, modal_force)


def solution(mesh):
    return jax.shard_map(
        on_device,
        mesh=mesh,
        in_specs=(
            P(None, "vert", "span", "stream"),
            P("vert", "span", "stream"),
            P(("stream", "span", "vert"), None, None),
            P(("stream", "span", "vert"), None),
            P("vert", "span", "stream", None),
            P("vert", None, "stream", None, None),
            P("vert", None, "stream", None),
            P(),
        ),
        out_specs=(P(None, "vert", "span", "stream"), P()),
        check_vma=False,
    )
```

profile of v0, /device:TPU:64, one launch (start us, length us, event | category | flops | bytes accessed | tf_op | source)
XLA Modules:
  0.0 263.3 jit_solution(5278629360200519969)
XLA Ops:
  0.6 2.2 fusion.52
  5.3 4.5 %collective-permute-start.1 = (f32[5,32,16,1]{1,2,3,0:T(8,128)S(1)}, f32[5,32,16,1]{1,2,3,0:T(8,128)S(1)}, u32[]{:S(2)}, u32[]{:S(2)}) collective-permute-start(f32[5,32,16,1]{1,2,3,0:T(8,128)S(1)} %copy.56), channel_id=1, source_target_pairs={{0,64},{64,128},{128,192},{192,256},{256,320},{320,384},{384,448},... | collective-permute-start | bytes 30728 | tf_op jit(solution)/shard_map/ppermute | solution.py:24
  12.2 13.3 %all-to-all-start = ((f32[64,1,2560]{2,1,0:T(1,128)}), f32[64,1,2560]{2,1,0:T(1,128)}, u32[]{:S(2)}, u32[]{:S(2)}) async-start(f32[64,1,2560]{2,1,0:T(1,128)} %all_to_all.8), calls=%async_computation | async-start | bytes 1310720 | tf_op jit(solution)/shard_map/all_to_all | solution.py:128
  30.7 2.5 pad_maximum_fusion.39
  33.2 2.0 collective-permute-start.2
  35.2 2.3 collective-permute-start.3
  37.5 4.0 %collective-permute-done.2 = f32[5,32,1,130]{3,2,1,0:T(1,128)S(1)} collective-permute-done((f32[5,32,1,130]{3,2,1,0:T(1,128)S(1)}, f32[5,32,1,130]{3,2,1,0:T(1,128)S(1)}, u32[]{:S(2)}, u32[]{:S(2)}) %collective-permute-start.2) | collective-permute-done | bytes 83232 | tf_op jit(solution)/shard_map/ppermute | solution.py:27
  44.5 4.7 %collective-permute-start.5 = (f32[5,1,18,130]{3,2,1,0:T(8,128)S(1)}, f32[5,1,18,130]{3,2,1,0:T(8,128)S(1)}, u32[]{:S(2)}, u32[]{:S(2)}) collective-permute-start(f32[5,1,18,130]{3,2,1,0:T(8,128)S(1)} %get-tuple-element.71), channel_id=1, source_target_pairs={{0,1},{1,2},{2,3},{4,5},{5,6},{6,7},{8,9},{9,10},{10,11},{12,13},{... | collective-permute-start | bytes 140408 | tf_op jit(solution)/shard_map/ppermute | solution.py:24
  51.7 3.2 %broadcast_multiply_fusion.3 = (f32[5,32,16,128]{3,2,1,0:T(8,128)S(1)}, f32[5,32,16,128]{3,2,1,0:T(8,128)S(1)}) fusion(f32[5,1,18,130]{3,2,1,0:T(8,128)S(1)} %collective-permute-done.4, f32[5,32,1,130]{3,2,1,0:T(1,128)S(1)} %collective-permute-done.2, f32[5,32,16,1]{3,2,1,0:T(8,128)S(1)} %copy.37, f32[5,32,16,128]{3,2,1,0:T(8,128)S(1)} %copy-done.1, ...), kind=kLoop, calls=%fused_computation.50 | loop fusion | flops 5242880 | bytes 4212640 | tf_op jit(solution)/shard_map/mul | solution.py:59
  58.7 2.6 %reduce = f32[64,2560]{1,0:T(8,128)S(1)} reduce(f32[64,1,2560]{2,1,0:T(1,128)} %all-to-all-done, f32[]{:T(128)} %constant.123), dimensions={1}, to_apply=%all_to_all.7.reduce_sub_computation | reduce | bytes 1310724 | tf_op jit(solution)/shard_map/all_to_all | solution.py:128
  63.1 30.8 %psum.14 = f32[5,32,16]{2,1,0:T(8,128)S(1)} all-reduce(f32[5,32,16]{2,1,0:T(8,128)S(1)} %reshape.200), channel_id=1, replica_groups=mesh['stream'=8,'span'=16,'vert'=4] {'stream'}, use_global_device_ids=true, to_apply=%region_3.4 | all-reduce | flops 2560 | bytes 20480 | tf_op jit(solution)/shard_map/psum | solution.py:144
  94.0 7.5 %multiply_add_fusion = f32[5,32,16,128]{3,2,1,0:T(8,128)S(1)} fusion(f32[5,32,16,128]{3,2,1,0:T(8,128)S(1)} %copy-done.1, f32[5,32,16,128]{3,2,1,0:T(8,128)} %broadcast_dynamic-update-slice_fusion.1, f32[5,32,16]{2,1,0:T(8,128)S(1)} %broadcast_add_fusion.1, f32[128]{0:T(128)S(1)} %compare_select_fusion.1, f32[32,16,128]{2,1,0:T(8,128)} %get-tuple-element.87, ...), kind=kLoop, calls=%fused_computation.45 | loop fusion | flops 13434880 | bytes 5009844 | tf_op jit(solution)/shard_map/add | solution.py:155
  108.5 4.5 %collective-permute-start.7 = (f32[5,32,16,1]{1,2,3,0:T(8,128)S(1)}, f32[5,32,16,1]{1,2,3,0:T(8,128)S(1)}, u32[]{:S(2)}, u32[]{:S(2)}) collective-permute-start(f32[5,32,16,1]{1,2,3,0:T(8,128)S(1)} %copy.46), channel_id=1, source_target_pairs={{0,64},{64,128},{128,192},{192,256},{256,320},{320,384},{384,448},... | collective-permute-start | bytes 30728 | tf_op jit(solution)/shard_map/ppermute | solution.py:24
  116.4 2.9 %pad_maximum_fusion.36 = (f32[5,32,1,130]{3,2,1,0:T(1,128)S(1)}, f32[5,32,1,130]{3,2,1,0:T(1,128)S(1)}) fusion(f32[5,32,16,1]{3,2,1,0:T(8,128)} %copy.45, f32[5,32,16,128]{3,2,1,0:T(8,128)S(1)} %multiply_add_fusion, f32[5,32,16,1]{3,2,1,0:T(8,128)} %copy.47), kind=kLoop, calls=%fused_computation.118 | loop fusion | flops 83200 | bytes 1497600 | tf_op jit(solution)/shard_map/concatenate | solution.py:28
  119.3 2.1 collective-permute-start.8
  121.4 2.6 collective-permute-start.9
  124.2 3.8 %collective-permute-done.9 = f32[5,32,1,130]{3,2,1,0:T(1,128)S(1)} collective-permute-done((f32[5,32,1,130]{3,2,1,0:T(1,128)S(1)}, f32[5,32,1,130]{3,2,1,0:T(1,128)S(1)}, u32[]{:S(2)}, u32[]{:S(2)}) %collective-permute-start.9) | collective-permute-done | bytes 83232 | tf_op jit(solution)/shard_map/ppermute | solution.py:24
  129.5 5.0 %collective-permute-start.11 = (f32[5,1,18,130]{3,2,1,0:T(8,128)S(1)}, f32[5,1,18,130]{3,2,1,0:T(8,128)S(1)}, u32[]{:S(2)}, u32[]{:S(2)}) collective-permute-start(f32[5,1,18,130]{3,2,1,0:T(8,128)S(1)} %get-tuple-element.69), channel_id=1, source_target_pairs={{0,1},{1,2},{2,3},{4,5},{5,6},{6,7},{8,9},{9,10},{10,11},{12,13},{... | collective-permute-start | bytes 140408 | tf_op jit(solution)/shard_map/ppermute | solution.py:24
  136.9 3.1 %broadcast_multiply_fusion = (f32[5,32,16,128]{3,2,1,0:T(8,128)S(1)}, f32[5,32,16,128]{3,2,1,0:T(8,128)S(1)}) fusion(f32[5,1,18,130]{3,2,1,0:T(8,128)S(1)} %collective-permute-done.10, f32[5,32,1,130]{3,2,1,0:T(1,128)S(1)} %collective-permute-done.8, f32[5,32,16,1]{3,2,1,0:T(8,128)S(1)} %copy-done.4, f32[5,32,16,128]{3,2,1,0:T(8,128)S(1)} %multiply_add_fusion, ...), kind=kLoop, calls=%fused_computation.47 | loop fusion | flops 5242880 | bytes 4212640 | tf_op jit(solution)/shard_map/mul | solution.py:59
  140.4 5.0 %add_multiply_fusion = f32[5,32,16,128]{3,2,1,0:T(8,128)S(1)} fusion(f32[5,32,16,128]{3,2,1,0:T(8,128)S(1)} %broadcast_dynamic-update-slice_fusion, f32[5,32,16,128]{3,2,1,0:T(8,128)S(1)} %multiply_add_fusion, f32[5,32,16,128]{3,2,1,0:T(8,128)S(1)} %copy-done.1, f32[32,16,128]{2,1,0:T(8,128)S(1)} %get-tuple-element.82, ...), kind=kLoop, calls=%fused_computation.44 | loop fusion | flops 14090240 | bytes 6320564 | tf_op jit(solution)/shard_map/mul | solution.py:157
  146.5 11.8 %gather_fusion = f32[2048]{0:T(1024)S(1)} fusion(f32[65536]{0:T(1024)S(1)} %bitcast.150, s32[2048]{0:T(1024)S(1)} %broadcast_clamp_fusion), kind=kCustom, calls=%fused_computation | custom fusion | bytes 24576 | tf_op jit(solution)/shard_map/gather | solution.py:159
  158.2 16.8 %all-gather = f32[32768]{0:T(1024)S(1)} all-gather(f32[2048]{0:T(1024)S(1)} %gather_fusion), channel_id=2, replica_groups=mesh['stream'=8,'span'=16,'vert'=4] {'span'}, dimensions={0}, use_global_device_ids=true | all-gather | bytes 139264 | tf_op jit(solution)/shard_map/all_gather | solution.py:161
  175.2 10.6 %while.11 = (s32[]{:T(128)}, f32[3,64]{1,0:T(4,128)S(1)}, f32[16,3,2048]{2,0,1:T(8,128)S(1)}, s32[16,2048]{1,0:T(8,128)S(1)}, s32[]{:T(128)}, /*index=5*/s32[]{:T(128)}) while((s32[]{:T(128)}, f32[3,64]{1,0:T(4,128)S(1)}, f32[16,3,2048]{2,0,1:T(8,128)S(1)}, s32[16,2048]{1,0:T(8,128)S(1)}, s32[]{:T(128)}, /*index=5*/s32[]{:T(128)}) %tuple.46), condition=%wide.region_5.6_spmd.clone, body=%wide.region_4.5_spmd.clone.sunk | while | flops 4850051 | bytes 99927 | solution.py:104
  186.0 77.3 %psum.15 = f32[32]{0:T(128)} all-reduce(f32[32]{0:T(128)S(1)} %convolution_bitcast_fusion), channel_id=1, replica_groups=mesh['stream'=8,'span'=16,'vert'=4] {'stream','vert'}, use_global_device_ids=true, to_apply=%region_6.7 | all-reduce | flops 32 | bytes 256 | tf_op jit(solution)/shard_map/psum | solution.py:165
  (152 shorter events, 46.9 us)
Async XLA Ops:
  0.6 185.2 %copy-start = (f32[3,64,32]{1,2,0:T(8,128)S(1)}, f32[3,64,32]{1,2,0:T(8,128)}, u32[]{:S(2)}) copy-start(f32[3,64,32]{1,2,0:T(8,128)} %param.20) | copy-start | bytes 73732
  3.4 25.0 %collective-permute-start = (f32[5,32,16,1]{1,2,3,0:T(8,128)S(1)}, f32[5,32,16,1]{1,2,3,0:T(8,128)S(1)}, u32[]{:S(2)}, u32[]{:S(2)}) collective-permute-start(f32[5,32,16,1]{1,2,3,0:T(8,128)S(1)} %copy.55), channel_id=1, source_target_pairs={{64,0},{128,64},{192,128},{256,192},{320,256},{384,320},{448,384},... | collective-permute-start | bytes 30728 | tf_op jit(solution)/shard_map/ppermute | solution.py:27
  5.3 23.7 %collective-permute-start.1 = (f32[5,32,16,1]{1,2,3,0:T(8,128)S(1)}, f32[5,32,16,1]{1,2,3,0:T(8,128)S(1)}, u32[]{:S(2)}, u32[]{:S(2)}) collective-permute-start(f32[5,32,16,1]{1,2,3,0:T(8,128)S(1)} %copy.56), channel_id=1, source_target_pairs={{0,64},{64,128},{128,192},{192,256},{256,320},{320,384},{384,448},... | collective-permute-start | bytes 30728 | tf_op jit(solution)/shard_map/ppermute | solution.py:24
  10.7 14.8 %copy-start.1 = (f32[5,32,16,128]{3,2,1,0:T(8,128)S(1)}, f32[5,32,16,128]{3,2,1,0:T(8,128)}, u32[]{:S(2)}) copy-start(f32[5,32,16,128]{3,2,1,0:T(8,128)} %param.13) | copy-start | bytes 3932164
  12.2 14.2 %copy-start.13 = (s32[1,1,1,2048]{3,2,1,0:T(1,128)S(1)}, s32[1,1,1,2048]{3,2,1,0:T(1,128)}, u32[]{:S(2)}) copy-start(s32[1,1,1,2048]{3,2,1,0:T(1,128)} %param.17) | copy-start | bytes 24580
  12.2 46.5 %all-to-all-start = ((f32[64,1,2560]{2,1,0:T(1,128)}), f32[64,1,2560]{2,1,0:T(1,128)}, u32[]{:S(2)}, u32[]{:S(2)}) async-start(f32[64,1,2560]{2,1,0:T(1,128)} %all_to_all.8), calls=%async_computation | async-start | bytes 1310720 | tf_op jit(solution)/shard_map/all_to_all | solution.py:128
  29.1 22.7 %copy-start.2 = (f32[5,32,16,1]{3,2,1,0:T(8,128)}, f32[5,32,16,1]{3,2,1,0:T(8,128)S(1)}, u32[]{:S(2)}) copy-start(f32[5,32,16,1]{3,2,1,0:T(8,128)S(1)} %copy.37) | copy-start | bytes 30724
  30.7 12.4 %copy-start.3 = (f32[5,32,16,1]{3,2,1,0:T(8,128)S(1)}, f32[5,32,16,1]{3,2,1,0:T(8,128)}, u32[]{:S(2)}) copy-start(f32[5,32,16,1]{3,2,1,0:T(8,128)} %copy.39) | copy-start | bytes 30724
  33.2 8.4 %collective-permute-start.2 = (f32[5,32,1,130]{3,2,1,0:T(1,128)S(1)}, f32[5,32,1,130]{3,2,1,0:T(1,128)S(1)}, u32[]{:S(2)}, u32[]{:S(2)}) collective-permute-start(f32[5,32,1,130]{3,2,1,0:T(1,128)S(1)} %get-tuple-element.80), channel_id=1, source_target_pairs={{4,0},{8,4},{12,8},{16,12},{20,16},{24,20},{28,24},{32,28},{36,32}... | collective-permute-start | bytes 249608 | tf_op jit(solution)/shard_map/ppermute | solution.py:27
  35.2 7.9 %collective-permute-start.3 = (f32[5,32,1,130]{3,2,1,0:T(1,128)S(1)}, f32[5,32,1,130]{3,2,1,0:T(1,128)S(1)}, u32[]{:S(2)}, u32[]{:S(2)}) collective-permute-start(f32[5,32,1,130]{3,2,1,0:T(1,128)S(1)} %get-tuple-element.79), channel_id=1, source_target_pairs={{0,4},{4,8},{8,12},{12,16},{16,20},{20,24},{24,28},{28,32},{32,36}... | collective-permute-start | bytes 249608 | tf_op jit(solution)/shard_map/ppermute | solution.py:24
  43.2 7.3 %collective-permute-start.4 = (f32[5,1,18,130]{3,2,1,0:T(8,128)S(1)}, f32[5,1,18,130]{3,2,1,0:T(8,128)S(1)}, u32[]{:S(2)}, u32[]{:S(2)}) collective-permute-start(f32[5,1,18,130]{3,2,1,0:T(8,128)S(1)} %get-tuple-element.72), channel_id=1, source_target_pairs={{1,0},{2,1},{3,2},{5,4},{6,5},{7,6},{9,8},{10,9},{11,10},{13,12},{... | collective-permute-start | bytes 140408 | tf_op jit(solution)/shard_map/ppermute | solution.py:27
  44.5 7.2 %collective-permute-start.5 = (f32[5,1,18,130]{3,2,1,0:T(8,128)S(1)}, f32[5,1,18,130]{3,2,1,0:T(8,128)S(1)}, u32[]{:S(2)}, u32[]{:S(2)}) collective-permute-start(f32[5,1,18,130]{3,2,1,0:T(8,128)S(1)} %get-tuple-element.71), channel_id=1, source_target_pairs={{0,1},{1,2},{2,3},{4,5},{5,6},{6,7},{8,9},{9,10},{10,11},{12,13},{... | collective-permute-start | bytes 140408 | tf_op jit(solution)/shard_map/ppermute | solution.py:24
  61.3 32.6 %copy-start.16 = (f32[5]{0:T(128)S(1)}, f32[5]{0:T(128)}, u32[]{:S(2)}) copy-start(f32[5]{0:T(128)} %constant.116.clone) | copy-start | bytes 64
  61.4 32.6 %copy-start.15 = (f32[5]{0:T(128)S(1)}, f32[5]{0:T(128)}, u32[]{:S(2)}) copy-start(f32[5]{0:T(128)} %constant.117.clone) | copy-start | bytes 64
  103.5 9.7 %copy-start.12 = (s32[1,16,1,2048]{3,2,1,0:T(1,128)S(1)}, s32[1,16,1,2048]{3,2,1,0:T(1,128)}, u32[]{:S(2)}) copy-start(s32[1,16,1,2048]{3,2,1,0:T(1,128)} %param.19) | copy-start | bytes 393220
  105.4 7.8 %collective-permute-start.6 = (f32[5,32,16,1]{1,2,3,0:T(8,128)S(1)}, f32[5,32,16,1]{1,2,3,0:T(8,128)S(1)}, u32[]{:S(2)}, u32[]{:S(2)}) collective-permute-start(f32[5,32,16,1]{1,2,3,0:T(8,128)S(1)} %copy.44), channel_id=1, source_target_pairs={{64,0},{128,64},{192,128},{256,192},{320,256},{384,320},{448,384},... | collective-permute-start | bytes 30728 | tf_op jit(solution)/shard_map/ppermute | solution.py:27
  108.5 6.3 %collective-permute-start.7 = (f32[5,32,16,1]{1,2,3,0:T(8,128)S(1)}, f32[5,32,16,1]{1,2,3,0:T(8,128)S(1)}, u32[]{:S(2)}, u32[]{:S(2)}) collective-permute-start(f32[5,32,16,1]{1,2,3,0:T(8,128)S(1)} %copy.46), channel_id=1, source_target_pairs={{0,64},{64,128},{128,192},{192,256},{256,320},{320,384},{384,448},... | collective-permute-start | bytes 30728 | tf_op jit(solution)/shard_map/ppermute | solution.py:24
  116.4 11.6 %copy-start.5 = (f32[5,32,16,1]{3,2,1,0:T(8,128)S(1)}, f32[5,32,16,1]{3,2,1,0:T(8,128)}, u32[]{:S(2)}) copy-start(f32[5,32,16,1]{3,2,1,0:T(8,128)} %copy.47) | copy-start | bytes 30724
  119.3 8.7 %copy-start.4 = (f32[5,32,16,1]{3,2,1,0:T(8,128)S(1)}, f32[5,32,16,1]{3,2,1,0:T(8,128)}, u32[]{:S(2)}) copy-start(f32[5,32,16,1]{3,2,1,0:T(8,128)} %copy.45) | copy-start | bytes 30724
  119.3 4.9 %collective-permute-start.8 = (f32[5,32,1,130]{3,2,1,0:T(1,128)S(1)}, f32[5,32,1,130]{3,2,1,0:T(1,128)S(1)}, u32[]{:S(2)}, u32[]{:S(2)}) collective-permute-start(f32[5,32,1,130]{3,2,1,0:T(1,128)S(1)} %get-tuple-element.76), channel_id=1, source_target_pairs={{4,0},{8,4},{12,8},{16,12},{20,16},{24,20},{28,24},{32,28},{36,32}... | collective-permute-start | bytes 249608 | tf_op jit(solution)/shard_map/ppermute | solution.py:27
  121.4 6.6 %collective-permute-start.9 = (f32[5,32,1,130]{3,2,1,0:T(1,128)S(1)}, f32[5,32,1,130]{3,2,1,0:T(1,128)S(1)}, u32[]{:S(2)}, u32[]{:S(2)}) collective-permute-start(f32[5,32,1,130]{3,2,1,0:T(1,128)S(1)} %get-tuple-element.75), channel_id=1, source_target_pairs={{0,4},{4,8},{8,12},{12,16},{16,20},{20,24},{24,28},{28,32},{32,36}... | collective-permute-start | bytes 249608 | tf_op jit(solution)/shard_map/ppermute | solution.py:24
  128.2 7.4 %collective-permute-start.10 = (f32[5,1,18,130]{3,2,1,0:T(8,128)S(1)}, f32[5,1,18,130]{3,2,1,0:T(8,128)S(1)}, u32[]{:S(2)}, u32[]{:S(2)}) collective-permute-start(f32[5,1,18,130]{3,2,1,0:T(8,128)S(1)} %get-tuple-element.70), channel_id=1, source_target_pairs={{1,0},{2,1},{3,2},{5,4},{6,5},{7,6},{9,8},{10,9},{11,10},{13,12},{... | collective-permute-start | bytes 140408 | tf_op jit(solution)/shard_map/ppermute | solution.py:27
  129.5 7.4 %collective-permute-start.11 = (f32[5,1,18,130]{3,2,1,0:T(8,128)S(1)}, f32[5,1,18,130]{3,2,1,0:T(8,128)S(1)}, u32[]{:S(2)}, u32[]{:S(2)}) collective-permute-start(f32[5,1,18,130]{3,2,1,0:T(8,128)S(1)} %get-tuple-element.69), channel_id=1, source_target_pairs={{0,1},{1,2},{2,3},{4,5},{5,6},{6,7},{8,9},{9,10},{10,11},{12,13},{... | collective-permute-start | bytes 140408 | tf_op jit(solution)/shard_map/ppermute | solution.py:24
  146.4 28.6 %copy-start.10 = (f32[1,16,1,3,2048]{4,2,3,1,0:T(1,128)S(1)}, f32[1,16,1,3,2048]{4,2,3,1,0:T(1,128)}, u32[]{:S(2)}) copy-start(f32[1,16,1,3,2048]{4,2,3,1,0:T(1,128)} %param.18) | copy-start | bytes 1179652
  (6 other events, 27.6 us)
where the time goes:
time: 264 us; the launch traced here: 263 us
  blocking collectives  125 us (47%)
  starting transfers between devices  46.3 us (18%)
  other arithmetic  36.1 us (14%)
  local copies, waits for them, and re-layouts  30.7 us (12%)
  waiting for transfers between devices  12.1 us (5%)
  matrix products  11.3 us (4%)
    psum x1, blocking collectives, on_device(): modal_force = lax.psum(modal_part, ('stream', 'vert'))  77.3 us
    psum x1, blocking collectives, on_device(): lax.psum(partial_value, 'stream').reshape(5, depth_cells, span_cells)  30.8 us
    ppermute x6, starting transfers between devices, extended(): lax.ppermute(lax.slice_in_dim(block, block.shape[dim] - width, None, axis...  23.8 us
    all_gather x1, blocking collectives, on_device(): lax.all_gather(sampled.reshape(1, 1, 1, -1), 'span', axis=1, tiled=True)  16.8 us
    all_to_all x1, starting transfers between devices, on_device(): lax.all_to_all(outgoing.reshape(tile_count, CAP * 5 * spec_cols), ('span'...  13.3 us
    gather x1, local copies, waits for them, and re-layouts, on_device(): sampled = pressure[deck_cells[0, 0, 0]]  11.8 us
    dot_general x16, matrix products, add_row(): jnp.dot(row_values, member, precision=lax.Precision.HIGHEST)  9.31 us
    ppermute x6, starting transfers between devices, extended(): lax.ppermute(lax.slice_in_dim(block, 0, width, axis=dim), axis, backward)  9.23 us
  transfers between devices with their start and end apart: 13, of which 7 were waited for; matrix products, arithmetic and copies ran while one was open for 8% of the time, Pallas kernels for 0%

commit v1 on v0

--- a/solution.py
+++ b/solution.py
@@ -14,6 +14,27 @@
 relax_time = 0.5
 relax_depth = 8.0
 wave_cols = 16
+
+
+def gather_around(x, axis, dim):
+    length, index, rows = (lax.axis_size(axis), lax.axis_index(axis), x.shape[dim])
+    right = [(i, (i + 1) % length) for i in range(length)]
+    left = [(i, (i - 1) % length) for i in range(length)]
+    result = jnp.zeros((*x.shape[:dim], length * rows, *x.shape[dim + 1 :]), x.dtype)
+    result = lax.dynamic_update_slice_in_dim(result, x, index * rows, axis=dim)
+    from_left = from_right = x
+    half = length // 2
+    for step in range(1, half + 1):
+        from_left = lax.ppermute(from_left, axis, right)
+        result = lax.dynamic_update_slice_in_dim(
+            result, from_left, (index - step) % length * rows, axis=dim
+        )
+        if step < length - half:
+            from_right = lax.ppermute(from_right, axis, left)
+            result = lax.dynamic_update_slice_in_dim(
+                result, from_right, (index + step) % length * rows, axis=dim
+            )
+    return result
 
 
 def extended(block, sides, width):
@@ -158,7 +179,7 @@
     pressure = new_fields[3].reshape(-1)
     sampled = pressure[deck_cells[0, 0, 0]]
     strip_count = mode_shapes.shape[1]
-    rows_all = lax.all_gather(sampled.reshape(1, 1, 1, -1), "span", axis=1, tiled=True)
+    rows_all = gather_around(sampled.reshape(1, 1, 1, -1), "span", 1)
     traction = rows_all[0, :, 0][:, None, :] * deck_geom[0, :, 0]
     forces = strip_forces(traction, strip_ids[0, :, 0], strip_count)
     modal_part = jnp.einsum("cj,cjm->m", forces, mode_shapes, precision=lax.Precision.HIGHEST)

time: 264 us -> 278 us (1.053)
  the two profiles are of different devices: /device:TPU:64 before, /device:TPU:256 now
where the time goes in v1:
time: 278 us; the launch traced here: 277 us
  blocking collectives  108 us (39%)
  starting transfers between devices  64.1 us (23%)
  local copies, waits for them, and re-layouts  34.3 us (12%)
  other arithmetic  33.3 us (12%)
  waiting for transfers between devices  23.7 us (9%)
  matrix products  11.3 us (4%)
    psum x1, blocking collectives, on_device(): modal_force = lax.psum(modal_part, ('stream', 'vert'))  77.4 us
    psum x1, blocking collectives, on_device(): lax.psum(partial_value, 'stream').reshape(5, depth_cells, span_cells)  30.8 us
    ppermute x6, starting transfers between devices, extended(): lax.ppermute(lax.slice_in_dim(block, block.shape[dim] - width, None, axis...  23.6 us
    ppermute x7, starting transfers between devices, gather_around(): from_right = lax.ppermute(from_right, axis, left)  20.5 us
    gather x1, local copies, waits for them, and re-layouts, on_device(): sampled = pressure[deck_cells[0, 0, 0]]  11.8 us
    all_to_all x1, starting transfers between devices, on_device(): lax.all_to_all(outgoing.reshape(tile_count, CAP * 5 * spec_cols), ('span'...  10.7 us
    ppermute x8, waiting for transfers between devices, gather_around(): from_left = lax.ppermute(from_left, axis, right)  10.2 us
    ppermute x6, starting transfers between devices, extended(): lax.ppermute(lax.slice_in_dim(block, 0, width, axis=dim), axis, backward)  9.38 us
  transfers between devices with their start and end apart: 28, of which 14 were waited for; matrix products, arithmetic and copies ran while one was open for 8% of the time, Pallas kernels for 0%

profile of v1, /device:TPU:256, one launch (start us, length us, event | category | flops | bytes accessed | tf_op | source)
XLA Modules:
  0.0 277.0 jit_solution(17347569069101850310)
XLA Ops:
  5.3 4.5 %collective-permute-start.1 = (f32[5,32,16,1]{1,2,3,0:T(8,128)S(1)}, f32[5,32,16,1]{1,2,3,0:T(8,128)S(1)}, u32[]{:S(2)}, u32[]{:S(2)}) collective-permute-start(f32[5,32,16,1]{1,2,3,0:T(8,128)S(1)} %copy.56), channel_id=1, source_target_pairs={{0,64},{64,128},{128,192},{192,256},{256,320},{320,384},{384,448},... | collective-permute-start | bytes 30728 | tf_op jit(solution)/shard_map/ppermute | solution.py:45
  12.2 10.7 %all-to-all-start = ((f32[64,1,2560]{2,1,0:T(1,128)}), f32[64,1,2560]{2,1,0:T(1,128)}, u32[]{:S(2)}, u32[]{:S(2)}) async-start(f32[64,1,2560]{2,1,0:T(1,128)} %all_to_all.8), calls=%async_computation | async-start | bytes 1310720 | tf_op jit(solution)/shard_map/all_to_all | solution.py:149
  34.9 4.0 %collective-permute-done.2 = f32[5,32,1,130]{3,2,1,0:T(1,128)S(1)} collective-permute-done((f32[5,32,1,130]{3,2,1,0:T(1,128)S(1)}, f32[5,32,1,130]{3,2,1,0:T(1,128)S(1)}, u32[]{:S(2)}, u32[]{:S(2)}) %collective-permute-start.2) | collective-permute-done | bytes 83232 | tf_op jit(solution)/shard_map/ppermute | solution.py:48
  42.1 4.7 %collective-permute-start.5 = (f32[5,1,18,130]{3,2,1,0:T(8,128)S(1)}, f32[5,1,18,130]{3,2,1,0:T(8,128)S(1)}, u32[]{:S(2)}, u32[]{:S(2)}) collective-permute-start(f32[5,1,18,130]{3,2,1,0:T(8,128)S(1)} %get-tuple-element.71), channel_id=1, source_target_pairs={{0,1},{1,2},{2,3},{4,5},{5,6},{6,7},{8,9},{9,10},{10,11},{12,13},{... | collective-permute-start | bytes 140408 | tf_op jit(solution)/shard_map/ppermute | solution.py:45
  49.0 3.2 %broadcast_multiply_fusion.3 = (f32[5,32,16,128]{3,2,1,0:T(8,128)S(1)}, f32[5,32,16,128]{3,2,1,0:T(8,128)S(1)}) fusion(f32[5,1,18,130]{3,2,1,0:T(8,128)S(1)} %collective-permute-done.4, f32[5,32,1,130]{3,2,1,0:T(1,128)S(1)} %collective-permute-done.2, f32[5,32,16,1]{3,2,1,0:T(8,128)S(1)} %copy.37, f32[5,32,16,128]{3,2,1,0:T(8,128)S(1)} %copy-done.1, ...), kind=kLoop, calls=%fused_computation.50 | loop fusion | flops 5242880 | bytes 4212640 | tf_op jit(solution)/shard_map/mul | solution.py:80
  53.6 2.6 reduce
  58.1 30.8 %psum.14 = f32[5,32,16]{2,1,0:T(8,128)S(1)} all-reduce(f32[5,32,16]{2,1,0:T(8,128)S(1)} %reshape.280), channel_id=1, replica_groups=mesh['stream'=8,'span'=16,'vert'=4] {'stream'}, use_global_device_ids=true, to_apply=%region_3.4 | all-reduce | flops 2560 | bytes 20480 | tf_op jit(solution)/shard_map/psum | solution.py:165
  88.9 7.5 %multiply_add_fusion = f32[5,32,16,128]{3,2,1,0:T(8,128)S(1)} fusion(f32[5,32,16,128]{3,2,1,0:T(8,128)S(1)} %copy-done.1, f32[5,32,16,128]{3,2,1,0:T(8,128)} %copy-done.8, f32[5,32,16]{2,1,0:T(8,128)S(1)} %broadcast_add_fusion.1, f32[128]{0:T(128)S(1)} %compare_select_fusion.1, f32[32,16,128]{2,1,0:T(8,128)} %get-tuple-element.87, ...), kind=kLoop, calls=%fused_computation.45 | loop fusion | flops 13434880 | bytes 5009844 | tf_op jit(solution)/shard_map/add | solution.py:176
  103.4 4.5 %collective-permute-start.7 = (f32[5,32,16,1]{1,2,3,0:T(8,128)S(1)}, f32[5,32,16,1]{1,2,3,0:T(8,128)S(1)}, u32[]{:S(2)}, u32[]{:S(2)}) collective-permute-start(f32[5,32,16,1]{1,2,3,0:T(8,128)S(1)} %copy.46), channel_id=1, source_target_pairs={{0,64},{64,128},{128,192},{192,256},{256,320},{320,384},{384,448},... | collective-permute-start | bytes 30728 | tf_op jit(solution)/shard_map/ppermute | solution.py:45
  111.3 2.9 %pad_maximum_fusion.36 = (f32[5,32,1,130]{3,2,1,0:T(1,128)S(1)}, f32[5,32,1,130]{3,2,1,0:T(1,128)S(1)}) fusion(f32[5,32,16,1]{3,2,1,0:T(8,128)} %copy.45, f32[5,32,16,128]{3,2,1,0:T(8,128)S(1)} %multiply_add_fusion, f32[5,32,16,1]{3,2,1,0:T(8,128)} %copy.47), kind=kLoop, calls=%fused_computation.118 | loop fusion | flops 83200 | bytes 1497600 | tf_op jit(solution)/shard_map/concatenate | solution.py:49
  119.0 5.0 %collective-permute-done.9 = f32[5,32,1,130]{3,2,1,0:T(1,128)S(1)} collective-permute-done((f32[5,32,1,130]{3,2,1,0:T(1,128)S(1)}, f32[5,32,1,130]{3,2,1,0:T(1,128)S(1)}, u32[]{:S(2)}, u32[]{:S(2)}) %collective-permute-start.9) | collective-permute-done | bytes 83232 | tf_op jit(solution)/shard_map/ppermute | solution.py:45
  125.5 5.0 %collective-permute-start.11 = (f32[5,1,18,130]{3,2,1,0:T(8,128)S(1)}, f32[5,1,18,130]{3,2,1,0:T(8,128)S(1)}, u32[]{:S(2)}, u32[]{:S(2)}) collective-permute-start(f32[5,1,18,130]{3,2,1,0:T(8,128)S(1)} %get-tuple-element.69), channel_id=1, source_target_pairs={{0,1},{1,2},{2,3},{4,5},{5,6},{6,7},{8,9},{9,10},{10,11},{12,13},{... | collective-permute-start | bytes 140408 | tf_op jit(solution)/shard_map/ppermute | solution.py:45
  132.9 3.1 %broadcast_multiply_fusion = (f32[5,32,16,128]{3,2,1,0:T(8,128)S(1)}, f32[5,32,16,128]{3,2,1,0:T(8,128)S(1)}) fusion(f32[5,1,18,130]{3,2,1,0:T(8,128)S(1)} %collective-permute-done.10, f32[5,32,1,130]{3,2,1,0:T(1,128)S(1)} %collective-permute-done.8, f32[5,32,16,1]{3,2,1,0:T(8,128)S(1)} %copy-done.4, f32[5,32,16,128]{3,2,1,0:T(8,128)S(1)} %multiply_add_fusion, ...), kind=kLoop, calls=%fused_computation.47 | loop fusion | flops 5242880 | bytes 4212640 | tf_op jit(solution)/shard_map/mul | solution.py:80
  136.4 5.0 %add_multiply_fusion = f32[5,32,16,128]{3,2,1,0:T(8,128)S(1)} fusion(f32[5,32,16,128]{3,2,1,0:T(8,128)S(1)} %broadcast_dynamic-update-slice_fusion, f32[5,32,16,128]{3,2,1,0:T(8,128)S(1)} %multiply_add_fusion, f32[5,32,16,128]{3,2,1,0:T(8,128)S(1)} %copy-done.1, f32[32,16,128]{2,1,0:T(8,128)S(1)} %get-tuple-element.82, ...), kind=kLoop, calls=%fused_computation.44 | loop fusion | flops 14090240 | bytes 6320564 | tf_op jit(solution)/shard_map/mul | solution.py:178
  142.5 11.8 %gather_fusion = f32[2048]{0:T(1024)S(1)} fusion(f32[65536]{0:T(1024)S(1)} %bitcast.167, s32[2048]{0:T(1024)S(1)} %broadcast_clamp_fusion), kind=kCustom, calls=%fused_computation | custom fusion | bytes 24576 | tf_op jit(solution)/shard_map/gather | solution.py:180
  154.3 2.9 %collective-permute-start.13 = (f32[1,1,1,2048]{3,2,1,0:T(1,128)S(1)}, f32[1,1,1,2048]{3,2,1,0:T(1,128)S(1)}, u32[]{:S(2)}, u32[]{:S(2)}) collective-permute-start(f32[1,1,1,2048]{3,2,1,0:T(1,128)S(1)} %bitcast.174), channel_id=1, source_target_pairs={{0,60},{4,0},{8,4},{12,8},{16,12},{20,16},{24,20},{28,24},{32,28},... | collective-permute-start | bytes 24584 | tf_op jit(solution)/shard_map/ppermute | solution.py:33
  158.6 2.9 %collective-permute-start.15 = (f32[1,1,1,2048]{3,2,1,0:T(1,128)S(1)}, f32[1,1,1,2048]{3,2,1,0:T(1,128)S(1)}, u32[]{:S(2)}, u32[]{:S(2)}) collective-permute-start(f32[1,1,1,2048]{3,2,1,0:T(1,128)S(1)} %collective-permute-done.13), channel_id=1, source_target_pairs={{0,60},{4,0},{8,4},{12,8},{16,12},{20,16},{24,20},{28,24},{32,28},... | collective-permute-start | bytes 24584 | tf_op jit(solution)/shard_map/ppermute | solution.py:33
  162.9 2.9 %collective-permute-start.17 = (f32[1,1,1,2048]{3,2,1,0:T(1,128)S(1)}, f32[1,1,1,2048]{3,2,1,0:T(1,128)S(1)}, u32[]{:S(2)}, u32[]{:S(2)}) collective-permute-start(f32[1,1,1,2048]{3,2,1,0:T(1,128)S(1)} %collective-permute-done.15), channel_id=1, source_target_pairs={{0,60},{4,0},{8,4},{12,8},{16,12},{20,16},{24,20},{28,24},{32,28},... | collective-permute-start | bytes 24584 | tf_op jit(solution)/shard_map/ppermute | solution.py:33
  167.2 2.9 %collective-permute-start.19 = (f32[1,1,1,2048]{3,2,1,0:T(1,128)S(1)}, f32[1,1,1,2048]{3,2,1,0:T(1,128)S(1)}, u32[]{:S(2)}, u32[]{:S(2)}) collective-permute-start(f32[1,1,1,2048]{3,2,1,0:T(1,128)S(1)} %collective-permute-done.17), channel_id=1, source_target_pairs={{0,60},{4,0},{8,4},{12,8},{16,12},{20,16},{24,20},{28,24},{32,28},... | collective-permute-start | bytes 24584 | tf_op jit(solution)/shard_map/ppermute | solution.py:33
  171.5 2.9 %collective-permute-start.21 = (f32[1,1,1,2048]{3,2,1,0:T(1,128)S(1)}, f32[1,1,1,2048]{3,2,1,0:T(1,128)S(1)}, u32[]{:S(2)}, u32[]{:S(2)}) collective-permute-start(f32[1,1,1,2048]{3,2,1,0:T(1,128)S(1)} %collective-permute-done.19), channel_id=1, source_target_pairs={{0,60},{4,0},{8,4},{12,8},{16,12},{20,16},{24,20},{28,24},{32,28},... | collective-permute-start | bytes 24584 | tf_op jit(solution)/shard_map/ppermute | solution.py:33
  175.7 2.9 %collective-permute-start.23 = (f32[1,1,1,2048]{3,2,1,0:T(1,128)S(1)}, f32[1,1,1,2048]{3,2,1,0:T(1,128)S(1)}, u32[]{:S(2)}, u32[]{:S(2)}) collective-permute-start(f32[1,1,1,2048]{3,2,1,0:T(1,128)S(1)} %collective-permute-done.21), channel_id=1, source_target_pairs={{0,60},{4,0},{8,4},{12,8},{16,12},{20,16},{24,20},{28,24},{32,28},... | collective-permute-start | bytes 24584 | tf_op jit(solution)/shard_map/ppermute | solution.py:33
  180.0 2.9 %collective-permute-start.25 = (f32[1,1,1,2048]{3,2,1,0:T(1,128)S(1)}, f32[1,1,1,2048]{3,2,1,0:T(1,128)S(1)}, u32[]{:S(2)}, u32[]{:S(2)}) collective-permute-start(f32[1,1,1,2048]{3,2,1,0:T(1,128)S(1)} %collective-permute-done.23), channel_id=1, source_target_pairs={{0,60},{4,0},{8,4},{12,8},{16,12},{20,16},{24,20},{28,24},{32,28},... | collective-permute-start | bytes 24584 | tf_op jit(solution)/shard_map/ppermute | solution.py:33
  188.9 10.6 %while.11 = (s32[]{:T(128)}, f32[3,64]{1,0:T(4,128)S(1)}, f32[16,3,2048]{2,0,1:T(8,128)S(1)}, s32[16,2048]{1,0:T(8,128)S(1)}, s32[]{:T(128)}, /*index=5*/s32[]{:T(128)}) while((s32[]{:T(128)}, f32[3,64]{1,0:T(4,128)S(1)}, f32[16,3,2048]{2,0,1:T(8,128)S(1)}, s32[16,2048]{1,0:T(8,128)S(1)}, s32[]{:T(128)}, /*index=5*/s32[]{:T(128)}) %tuple.46), condition=%wide.region_5.6_spmd.clone, body=%wide.region_4.5_spmd.clone.sunk | while | flops 4850051 | bytes 99927 | solution.py:125
  199.7 77.4 %psum.15 = f32[32]{0:T(128)} all-reduce(f32[32]{0:T(128)S(1)} %convolution_bitcast_fusion), channel_id=1, replica_groups=mesh['stream'=8,'span'=16,'vert'=4] {'stream','vert'}, use_global_device_ids=true, to_apply=%region_6.7 | all-reduce | flops 32 | bytes 256 | tf_op jit(solution)/shard_map/psum | solution.py:186
  (199 shorter events, 71.7 us)
Async XLA Ops:
  3.4 22.4 %collective-permute-start = (f32[5,32,16,1]{1,2,3,0:T(8,128)S(1)}, f32[5,32,16,1]{1,2,3,0:T(8,128)S(1)}, u32[]{:S(2)}, u32[]{:S(2)}) collective-permute-start(f32[5,32,16,1]{1,2,3,0:T(8,128)S(1)} %copy.55), channel_id=1, source_target_pairs={{64,0},{128,64},{192,128},{256,192},{320,256},{384,320},{448,384},... | collective-permute-start | bytes 30728 | tf_op jit(solution)/shard_map/ppermute | solution.py:48
  5.3 21.1 %collective-permute-start.1 = (f32[5,32,16,1]{1,2,3,0:T(8,128)S(1)}, f32[5,32,16,1]{1,2,3,0:T(8,128)S(1)}, u32[]{:S(2)}, u32[]{:S(2)}) collective-permute-start(f32[5,32,16,1]{1,2,3,0:T(8,128)S(1)} %copy.56), channel_id=1, source_target_pairs={{0,64},{64,128},{128,192},{192,256},{256,320},{320,384},{384,448},... | collective-permute-start | bytes 30728 | tf_op jit(solution)/shard_map/ppermute | solution.py:45
  12.2 41.4 %all-to-all-start = ((f32[64,1,2560]{2,1,0:T(1,128)}), f32[64,1,2560]{2,1,0:T(1,128)}, u32[]{:S(2)}, u32[]{:S(2)}) async-start(f32[64,1,2560]{2,1,0:T(1,128)} %all_to_all.8), calls=%async_computation | async-start | bytes 1310720 | tf_op jit(solution)/shard_map/all_to_all | solution.py:149
  30.6 8.4 %collective-permute-start.2 = (f32[5,32,1,130]{3,2,1,0:T(1,128)S(1)}, f32[5,32,1,130]{3,2,1,0:T(1,128)S(1)}, u32[]{:S(2)}, u32[]{:S(2)}) collective-permute-start(f32[5,32,1,130]{3,2,1,0:T(1,128)S(1)} %get-tuple-element.80), channel_id=1, source_target_pairs={{4,0},{8,4},{12,8},{16,12},{20,16},{24,20},{28,24},{32,28},{36,32}... | collective-permute-start | bytes 249608 | tf_op jit(solution)/shard_map/ppermute | solution.py:48
  32.7 7.8 %collective-permute-start.3 = (f32[5,32,1,130]{3,2,1,0:T(1,128)S(1)}, f32[5,32,1,130]{3,2,1,0:T(1,128)S(1)}, u32[]{:S(2)}, u32[]{:S(2)}) collective-permute-start(f32[5,32,1,130]{3,2,1,0:T(1,128)S(1)} %get-tuple-element.79), channel_id=1, source_target_pairs={{0,4},{4,8},{8,12},{12,16},{16,20},{20,24},{24,28},{28,32},{32,36}... | collective-permute-start | bytes 249608 | tf_op jit(solution)/shard_map/ppermute | solution.py:45
  40.8 7.2 %collective-permute-start.4 = (f32[5,1,18,130]{3,2,1,0:T(8,128)S(1)}, f32[5,1,18,130]{3,2,1,0:T(8,128)S(1)}, u32[]{:S(2)}, u32[]{:S(2)}) collective-permute-start(f32[5,1,18,130]{3,2,1,0:T(8,128)S(1)} %get-tuple-element.72), channel_id=1, source_target_pairs={{1,0},{2,1},{3,2},{5,4},{6,5},{7,6},{9,8},{10,9},{11,10},{13,12},{... | collective-permute-start | bytes 140408 | tf_op jit(solution)/shard_map/ppermute | solution.py:48
  42.1 7.0 %collective-permute-start.5 = (f32[5,1,18,130]{3,2,1,0:T(8,128)S(1)}, f32[5,1,18,130]{3,2,1,0:T(8,128)S(1)}, u32[]{:S(2)}, u32[]{:S(2)}) collective-permute-start(f32[5,1,18,130]{3,2,1,0:T(8,128)S(1)} %get-tuple-element.71), channel_id=1, source_target_pairs={{0,1},{1,2},{2,3},{4,5},{5,6},{6,7},{8,9},{9,10},{10,11},{12,13},{... | collective-permute-start | bytes 140408 | tf_op jit(solution)/shard_map/ppermute | solution.py:45
  100.3 7.7 %collective-permute-start.6 = (f32[5,32,16,1]{1,2,3,0:T(8,128)S(1)}, f32[5,32,16,1]{1,2,3,0:T(8,128)S(1)}, u32[]{:S(2)}, u32[]{:S(2)}) collective-permute-start(f32[5,32,16,1]{1,2,3,0:T(8,128)S(1)} %copy.44), channel_id=1, source_target_pairs={{64,0},{128,64},{192,128},{256,192},{320,256},{384,320},{448,384},... | collective-permute-start | bytes 30728 | tf_op jit(solution)/shard_map/ppermute | solution.py:48
  103.4 6.2 %collective-permute-start.7 = (f32[5,32,16,1]{1,2,3,0:T(8,128)S(1)}, f32[5,32,16,1]{1,2,3,0:T(8,128)S(1)}, u32[]{:S(2)}, u32[]{:S(2)}) collective-permute-start(f32[5,32,16,1]{1,2,3,0:T(8,128)S(1)} %copy.46), channel_id=1, source_target_pairs={{0,64},{64,128},{128,192},{192,256},{256,320},{320,384},{384,448},... | collective-permute-start | bytes 30728 | tf_op jit(solution)/shard_map/ppermute | solution.py:45
  114.2 4.9 %collective-permute-start.8 = (f32[5,32,1,130]{3,2,1,0:T(1,128)S(1)}, f32[5,32,1,130]{3,2,1,0:T(1,128)S(1)}, u32[]{:S(2)}, u32[]{:S(2)}) collective-permute-start(f32[5,32,1,130]{3,2,1,0:T(1,128)S(1)} %get-tuple-element.76), channel_id=1, source_target_pairs={{4,0},{8,4},{12,8},{16,12},{20,16},{24,20},{28,24},{32,28},{36,32}... | collective-permute-start | bytes 249608 | tf_op jit(solution)/shard_map/ppermute | solution.py:48
  116.2 7.8 %collective-permute-start.9 = (f32[5,32,1,130]{3,2,1,0:T(1,128)S(1)}, f32[5,32,1,130]{3,2,1,0:T(1,128)S(1)}, u32[]{:S(2)}, u32[]{:S(2)}) collective-permute-start(f32[5,32,1,130]{3,2,1,0:T(1,128)S(1)} %get-tuple-element.75), channel_id=1, source_target_pairs={{0,4},{4,8},{8,12},{12,16},{16,20},{20,24},{24,28},{28,32},{32,36}... | collective-permute-start | bytes 249608 | tf_op jit(solution)/shard_map/ppermute | solution.py:45
  124.2 7.4 %collective-permute-start.10 = (f32[5,1,18,130]{3,2,1,0:T(8,128)S(1)}, f32[5,1,18,130]{3,2,1,0:T(8,128)S(1)}, u32[]{:S(2)}, u32[]{:S(2)}) collective-permute-start(f32[5,1,18,130]{3,2,1,0:T(8,128)S(1)} %get-tuple-element.70), channel_id=1, source_target_pairs={{1,0},{2,1},{3,2},{5,4},{6,5},{7,6},{9,8},{10,9},{11,10},{13,12},{... | collective-permute-start | bytes 140408 | tf_op jit(solution)/shard_map/ppermute | solution.py:48
  125.5 7.4 %collective-permute-start.11 = (f32[5,1,18,130]{3,2,1,0:T(8,128)S(1)}, f32[5,1,18,130]{3,2,1,0:T(8,128)S(1)}, u32[]{:S(2)}, u32[]{:S(2)}) collective-permute-start(f32[5,1,18,130]{3,2,1,0:T(8,128)S(1)} %get-tuple-element.69), channel_id=1, source_target_pairs={{0,1},{1,2},{2,3},{4,5},{5,6},{6,7},{8,9},{9,10},{10,11},{12,13},{... | collective-permute-start | bytes 140408 | tf_op jit(solution)/shard_map/ppermute | solution.py:45
  154.3 4.3 %collective-permute-start.12 = (f32[1,1,1,2048]{3,2,1,0:T(1,128)S(1)}, f32[1,1,1,2048]{3,2,1,0:T(1,128)S(1)}, u32[]{:S(2)}, u32[]{:S(2)}) collective-permute-start(f32[1,1,1,2048]{3,2,1,0:T(1,128)S(1)} %bitcast.173), channel_id=1, source_target_pairs={{0,4},{4,8},{8,12},{12,16},{16,20},{20,24},{24,28},{28,32},{32,36}... | collective-permute-start | bytes 24584 | tf_op jit(solution)/shard_map/ppermute | solution.py:28
  154.3 4.3 %collective-permute-start.13 = (f32[1,1,1,2048]{3,2,1,0:T(1,128)S(1)}, f32[1,1,1,2048]{3,2,1,0:T(1,128)S(1)}, u32[]{:S(2)}, u32[]{:S(2)}) collective-permute-start(f32[1,1,1,2048]{3,2,1,0:T(1,128)S(1)} %bitcast.174), channel_id=1, source_target_pairs={{0,60},{4,0},{8,4},{12,8},{16,12},{20,16},{24,20},{28,24},{32,28},... | collective-permute-start | bytes 24584 | tf_op jit(solution)/shard_map/ppermute | solution.py:33
  158.6 4.3 %collective-permute-start.14 = (f32[1,1,1,2048]{3,2,1,0:T(1,128)S(1)}, f32[1,1,1,2048]{3,2,1,0:T(1,128)S(1)}, u32[]{:S(2)}, u32[]{:S(2)}) collective-permute-start(f32[1,1,1,2048]{3,2,1,0:T(1,128)S(1)} %collective-permute-done.12), channel_id=1, source_target_pairs={{0,4},{4,8},{8,12},{12,16},{16,20},{20,24},{24,28},{28,32},{32,36}... | collective-permute-start | bytes 24584 | tf_op jit(solution)/shard_map/ppermute | solution.py:28
  158.6 4.3 %collective-permute-start.15 = (f32[1,1,1,2048]{3,2,1,0:T(1,128)S(1)}, f32[1,1,1,2048]{3,2,1,0:T(1,128)S(1)}, u32[]{:S(2)}, u32[]{:S(2)}) collective-permute-start(f32[1,1,1,2048]{3,2,1,0:T(1,128)S(1)} %collective-permute-done.13), channel_id=1, source_target_pairs={{0,60},{4,0},{8,4},{12,8},{16,12},{20,16},{24,20},{28,24},{32,28},... | collective-permute-start | bytes 24584 | tf_op jit(solution)/shard_map/ppermute | solution.py:33
  162.8 4.3 %collective-permute-start.16 = (f32[1,1,1,2048]{3,2,1,0:T(1,128)S(1)}, f32[1,1,1,2048]{3,2,1,0:T(1,128)S(1)}, u32[]{:S(2)}, u32[]{:S(2)}) collective-permute-start(f32[1,1,1,2048]{3,2,1,0:T(1,128)S(1)} %collective-permute-done.14), channel_id=1, source_target_pairs={{0,4},{4,8},{8,12},{12,16},{16,20},{20,24},{24,28},{28,32},{32,36}... | collective-permute-start | bytes 24584 | tf_op jit(solution)/shard_map/ppermute | solution.py:28
  162.9 4.3 %collective-permute-start.17 = (f32[1,1,1,2048]{3,2,1,0:T(1,128)S(1)}, f32[1,1,1,2048]{3,2,1,0:T(1,128)S(1)}, u32[]{:S(2)}, u32[]{:S(2)}) collective-permute-start(f32[1,1,1,2048]{3,2,1,0:T(1,128)S(1)} %collective-permute-done.15), channel_id=1, source_target_pairs={{0,60},{4,0},{8,4},{12,8},{16,12},{20,16},{24,20},{28,24},{32,28},... | collective-permute-start | bytes 24584 | tf_op jit(solution)/shard_map/ppermute | solution.py:33
  167.1 4.3 %collective-permute-start.18 = (f32[1,1,1,2048]{3,2,1,0:T(1,128)S(1)}, f32[1,1,1,2048]{3,2,1,0:T(1,128)S(1)}, u32[]{:S(2)}, u32[]{:S(2)}) collective-permute-start(f32[1,1,1,2048]{3,2,1,0:T(1,128)S(1)} %collective-permute-done.16), channel_id=1, source_target_pairs={{0,4},{4,8},{8,12},{12,16},{16,20},{20,24},{24,28},{28,32},{32,36}... | collective-permute-start | bytes 24584 | tf_op jit(solution)/shard_map/ppermute | solution.py:28
  167.2 4.3 %collective-permute-start.19 = (f32[1,1,1,2048]{3,2,1,0:T(1,128)S(1)}, f32[1,1,1,2048]{3,2,1,0:T(1,128)S(1)}, u32[]{:S(2)}, u32[]{:S(2)}) collective-permute-start(f32[1,1,1,2048]{3,2,1,0:T(1,128)S(1)} %collective-permute-done.17), channel_id=1, source_target_pairs={{0,60},{4,0},{8,4},{12,8},{16,12},{20,16},{24,20},{28,24},{32,28},... | collective-permute-start | bytes 24584 | tf_op jit(solution)/shard_map/ppermute | solution.py:33
  171.4 4.3 %collective-permute-start.20 = (f32[1,1,1,2048]{3,2,1,0:T(1,128)S(1)}, f32[1,1,1,2048]{3,2,1,0:T(1,128)S(1)}, u32[]{:S(2)}, u32[]{:S(2)}) collective-permute-start(f32[1,1,1,2048]{3,2,1,0:T(1,128)S(1)} %collective-permute-done.18), channel_id=1, source_target_pairs={{0,4},{4,8},{8,12},{12,16},{16,20},{20,24},{24,28},{28,32},{32,36}... | collective-permute-start | bytes 24584 | tf_op jit(solution)/shard_map/ppermute | solution.py:28
  175.7 4.3 %collective-permute-start.22 = (f32[1,1,1,2048]{3,2,1,0:T(1,128)S(1)}, f32[1,1,1,2048]{3,2,1,0:T(1,128)S(1)}, u32[]{:S(2)}, u32[]{:S(2)}) collective-permute-start(f32[1,1,1,2048]{3,2,1,0:T(1,128)S(1)} %collective-permute-done.20), channel_id=1, source_target_pairs={{0,4},{4,8},{8,12},{12,16},{16,20},{20,24},{24,28},{28,32},{32,36}... | collective-permute-start | bytes 24584 | tf_op jit(solution)/shard_map/ppermute | solution.py:28
  180.0 7.4 %collective-permute-start.25 = (f32[1,1,1,2048]{3,2,1,0:T(1,128)S(1)}, f32[1,1,1,2048]{3,2,1,0:T(1,128)S(1)}, u32[]{:S(2)}, u32[]{:S(2)}) collective-permute-start(f32[1,1,1,2048]{3,2,1,0:T(1,128)S(1)} %collective-permute-done.23), channel_id=1, source_target_pairs={{0,60},{4,0},{8,4},{12,8},{16,12},{20,16},{24,20},{28,24},{32,28},... | collective-permute-start | bytes 24584 | tf_op jit(solution)/shard_map/ppermute | solution.py:33
  (22 other events, 467.6 us)
